TPU v7x, 32 devices: a whole 2x2x4 slice. The times are simulated.
32 devices in a mesh: grp: 2 (over y), tok: 16 (over z, x, core).
Axes of the slice: x: 2, y: 2, z: 4, core: 2. Of those that a mesh axis runs over, the one named last changes fastest.
Arguments:
- hidden: bfloat16 [4, 1024, 1536], P('grp', 'tok'), parts along dimension 0
- base_ids: int32 [4, 1024], P('grp', 'tok'), parts along dimension 0, may hold values from 0 to 4, as said below
- attn_gain: bfloat16 [1536], replicated, may hold values from 0.099609375 to 1.8984375
- q_weight: bfloat16 [1536, 768], replicated
- kv_weight: bfloat16 [1536, 384], replicated
- out_weight: bfloat16 [768, 1536], replicated, may hold values from -0.21875 to 0.21875
- head_gain: bfloat16 [1536], replicated, may hold values from 0.099609375 to 1.8984375
- head_weight: bfloat16 [1536, 1536], replicated, may hold values from -0.15625 to 0.15625
- head_bias: float32 [1536], replicated, may hold values from -1 to 1
- track_perm: int32 [1536], replicated, may hold values from 0 to 1535, each once
Outputs:
- combined: float32 [2048, 1536], P(('grp', 'tok')), parts along dimension 0
There are 2 independent parts, one for each index of `grp`. A program takes and returns all parts, laid end to end along the dimension named above; an argument that names none is the same for every part. Nothing has to cross between parts.
Inputs may be any that keep to these rules, and one draw needn't show every extreme that they name: `base_ids`: every eighth token of each strand, from token 0, has a base 0 to 3.
All inputs are finite; a program needn't handle non-finite values.
Results may differ from a plain program's by a relative error of at most 0.0058.
Values may be sent and summed in bfloat16 or wider, within the bound.
No kernel may reach another device: no remote copies, remote signals or barrier semaphores. Data moves between devices by JAX's collectives and lax.ppermute only.
A program may use at most 128 MiB of HBM per device.

v0:
```python
import math
import jax
import jax.numpy as jnp
from jax import lax
from jax.sharding import PartitionSpec as P


def swapped(value, axis, distance):
    mask = 2**distance
    pairs = [(source, source ^ mask) for source in range(lax.axis_size(axis))]
    return lax.ppermute(value, axis, pairs)


def normalize(rows, gain):
    widened = rows.astype(jnp.float32)
    return (
        widened
        * lax.rsqrt(jnp.mean(widened * widened, -1, keepdims=True) + 1e-06)
        * gain.astype(jnp.float32)
    )


def attend(running, queries, key_value, usable_flag):
    maxima, totals, accumulated = running
    width_head = queries.shape[2]
    key_rows = key_value[:, :, :width_head]
    value_rows = key_value[:, :, width_head:]
    scores = jnp.einsum("srd,skd->srk", queries, key_rows, preferred_element_type=jnp.float32) * (
        1.0 / math.sqrt(width_head)
    )
    usable = usable_flag[:, None, :] > 0
    scores = jnp.where(usable, scores, jnp.float32(-1e30))
    new_maxima = jnp.maximum(maxima, jnp.max(scores, -1))
    weight_exp = jnp.where(usable, jnp.exp(scores - new_maxima[:, :, None]), jnp.float32(0.0))
    totals = jnp.sum(weight_exp, -1)
    summed = jnp.einsum(
        "srk,skd->srd",
        weight_exp.astype(jnp.bfloat16),
        value_rows,
        preferred_element_type=jnp.float32,
    )
    accumulated = summed
    return (new_maxima, totals, accumulated)


def per_device(
    hidden,
    base_ids,
    attn_gain,
    q_weight,
    kv_weight,
    out_weight,
    head_gain,
    head_weight,
    head_bias,
    track_perm,
):
    tok_rows = hidden.shape[1]
    width_head = kv_weight.shape[1] // 2
    head_count = q_weight.shape[1] // width_head
    bit_count = lax.axis_size("tok").bit_length() - 1
    normed = normalize(hidden, attn_gain).astype(jnp.bfloat16)
    key_value = jnp.einsum(
        "std,de->ste", normed, kv_weight, preferred_element_type=jnp.float32
    ).astype(jnp.bfloat16)
    usable_flag = (base_ids != 4).astype(jnp.bfloat16)
    partner = hidden[1]
    for bit_number in range(bit_count):
        partner = swapped(partner, "tok", bit_number)
    partner = partner[::-1]
    query_source = jnp.stack([normed[0], normalize(partner, attn_gain).astype(jnp.bfloat16)])
    residual_base = jnp.stack([hidden[0], partner])
    queries = jnp.einsum(
        "std,de->ste", query_source, q_weight, preferred_element_type=jnp.float32
    ).astype(jnp.bfloat16)
    queries = queries.reshape(2, tok_rows * head_count, width_head)
    row_count = queries.shape[1]
    start_state = (
        jnp.full((2, row_count), -1e30, jnp.float32),
        jnp.zeros((2, row_count), jnp.float32),
        jnp.zeros((2, row_count, width_head), jnp.float32),
    )
    softmax_state = attend(
        start_state,
        queries,
        lax.all_gather(key_value, "tok", axis=1, tiled=True),
        lax.all_gather(usable_flag, "tok", axis=1, tiled=True),
    )
    maxima, totals, accumulated = softmax_state
    attended = (
        (accumulated / totals[:, :, None])
        .astype(jnp.bfloat16)
        .reshape(2, tok_rows, head_count * width_head)
    )
    residual_sum = residual_base.astype(jnp.float32) + jnp.einsum(
        "ste,ed->std", attended, out_weight, preferred_element_type=jnp.float32
    )
    normed_out = normalize(residual_sum, head_gain).astype(jnp.bfloat16)
    forward_logits = (
        jnp.dot(normed_out[0], head_weight, preferred_element_type=jnp.float32) + head_bias
    )
    reverse_logits = (
        jnp.dot(normed_out[1], head_weight[:, track_perm], preferred_element_type=jnp.float32)
        + head_bias[track_perm]
    )
    forward_pred = jax.nn.softplus(forward_logits).astype(jnp.bfloat16)
    reverse_pred = jax.nn.softplus(reverse_logits).astype(jnp.bfloat16)
    return 0.5 * (forward_pred.astype(jnp.float32) + reverse_pred.astype(jnp.float32))


def solution(mesh):
    placed = (P("grp", "tok", None), P("grp", "tok"), P(), P(), P(), P(), P(), P(), P(), P())
    return jax.shard_map(
        per_device, mesh=mesh, in_specs=placed, out_specs=P(("grp", "tok"), None), check_vma=False
    )
```

profile of v0, /device:TPU:0, one launch (start us, length us, event | category | flops | bytes accessed | tf_op | source)
XLA Modules:
  0.0 101.3 jit_solution(12420879725566651075)
XLA Ops:
  6.5 0.0 all-gather.3.cloned.1.call-start
  6.6 0.8 convert_element_type.55
  7.4 1.2 %fusion.25 = f32[2,64]{1,0:T(2,128)S(1)} fusion(bf16[2,64,1536]{2,1,0:T(8,128)(2,1)} %param.10), kind=kLoop, calls=%fused_computation.31 | loop fusion | flops 589696 | bytes 393728 | tf_op jit(solution)/shard_map/reduce_sum | solution.py:18
  8.6 1.2 %fusion.27 = bf16[2,64,1536]{2,1,0:T(8,128)(2,1)S(1)} fusion(bf16[2,64,1536]{2,1,0:T(8,128)(2,1)} %param.10, f32[1536]{0:T(1024)S(1)} %convert_element_type.55, f32[2,64]{1,0:T(2,128)S(1)} %add_rsqrt_fusion.1), kind=kLoop, calls=%fused_computation.33 | loop fusion | flops 786432 | bytes 793088 | tf_op jit(solution)/shard_map/convert_element_type | solution.py:62
  9.8 0.0 copy-start.3
  9.8 2.4 %fusion.13 = bf16[2,64,384]{2,1,0:T(8,128)(2,1)} fusion(bf16[2,64,1536]{2,1,0:T(8,128)(2,1)S(1)} %fusion.27, bf16[1536,384]{1,0:T(8,128)(2,1)} %param.14), kind=kOutput, calls=%fused_computation.20 | convolution fusion | flops 151044096 | bytes 1671168 | tf_op jit(solution)/shard_map/std,de->ste/dot_general | solution.py:63
  12.2 0.0 all-gather.3.cloned.1.call-update
  12.3 0.6 collective-permute-start
  12.8 1.1 %collective-permute-done = bf16[64,1536]{1,0:T(8,128)(2,1)S(1)} collective-permute-done((bf16[64,1536]{1,0:T(8,128)(2,1)S(1)}, bf16[64,1536]{1,0:T(8,128)(2,1)S(1)}, u32[]{:S(2)}, u32[]{:S(2)}) %collective-permute-start) | collective-permute-done | bytes 196640 | tf_op jit(solution)/shard_map/ppermute | solution.py:11
  13.9 2.8 %collective-permute-start.1 = (bf16[64,1536]{1,0:T(8,128)(2,1)S(1)}, bf16[64,1536]{1,0:T(8,128)(2,1)S(1)}, u32[]{:S(2)}, u32[]{:S(2)}) collective-permute-start(bf16[64,1536]{1,0:T(8,128)(2,1)S(1)} %collective-permute-done), channel_id=1, source_target_pairs={{0,2},{1,3},{2,0},{3,1},{4,6},{5,7},{6,4},{7,5},{8,10},{9,11},{10,... | collective-permute-start | bytes 589832 | tf_op jit(solution)/shard_map/ppermute | solution.py:11
  16.7 20.7 %all-gather = bf16[16,64,2]{1,2,0:T(2,128)(2,1)S(1)} all-gather(bf16[1,64,2]{1,2,0:T(2,128)(2,1)S(1)} %fusion.37), channel_id=1, replica_groups=mesh['grp'=2,'tok'=16] {'tok'}, dimensions={0}, use_global_device_ids=true | all-gather | bytes 4352 | tf_op jit(solution)/shard_map/all_gather | solution.py:87
  37.4 11.5 %collective-permute-done.2 = bf16[64,1536]{1,0:T(8,128)(2,1)} collective-permute-done((bf16[64,1536]{1,0:T(8,128)(2,1)S(1)}, bf16[64,1536]{1,0:T(8,128)(2,1)}, u32[]{:S(2)}, u32[]{:S(2)}) %collective-permute-start.2) | collective-permute-done | bytes 196640 | tf_op jit(solution)/shard_map/ppermute | solution.py:11
  48.9 0.0 copy-start.5
  48.9 6.7 %copy.26 = bf16[1536,1536]{0,1:T(8,128)(2,1)} copy(bf16[1536,1536]{1,0:T(8,128)(2,1)} %param.17) | data formatting | bytes 9437184 | tf_op args[7]
  55.7 0.1 reshape.64
  55.8 0.0 copy-start.1
  55.8 13.4 %gather_fusion = bf16[1536,1536]{1,0:T(8,128)(2,1)} fusion(bf16[1536,1536]{0,1:T(8,128)(2,1)} %copy.26, s32[2048]{0:T(1024)S(1)} %pad_clamp_fusion), kind=kCustom, calls=%fused_computation | custom fusion | bytes 9443328 | tf_op jit(solution)/shard_map/gather | solution.py:103
  69.2 8.4 %gather_fusion.1 = f32[1536]{0:T(1024)S(1)} fusion(f32[1536]{0:T(1024)S(1)} %copy-done.1, s32[2048]{0:T(1024)S(1)} %pad_clamp_fusion), kind=kCustom, calls=%fused_computation.1 | custom fusion | bytes 18432 | tf_op jit(solution)/shard_map/gather | solution.py:104
  77.6 0.3 rev.3
  77.9 0.1 fusion.28
  78.1 0.1 fusion.36
  78.2 2.2 %fusion.10 = bf16[2,64,768]{2,1,0:T(8,128)(2,1)S(1)} fusion(bf16[1536,768]{1,0:T(8,128)(2,1)} %param.13, bf16[1,64,1536]{2,1,0:T(8,128)(2,1)S(1)} %fusion.36, bf16[1,64,1536]{2,1,0:T(8,128)(2,1)S(1)} %slice-done), kind=kOutput, calls=%fused_computation.19 | convolution fusion | flops 302284800 | bytes 2949120 | tf_op jit(solution)/shard_map/std,de->ste/dot_general | solution.py:73
  80.4 1.0 reshape.41
  81.3 2.0 %fusion.4 = (f32[2,256]{1,0:T(2,128)S(1)}, f32[2,256,1024]{2,1,0:T(8,128)S(1)}) fusion(pred[2,1024]{1,0:T(4,128)(4,1)S(1)} %bitcast.40, bf16[2,256,192]{2,1,0:T(8,128)(2,1)} %reshape.41, bf16[2,1024,384]{2,1,0:T(8,128)(2,1)} %all-gather.3.cloned.1.call-done), kind=kOutput, calls=%fused_computation.10 | convolution fusion | flops 202898944 | bytes 3411968 | tf_op jit(solution)/shard_map/srd,skd->srk/dot_general | solution.py:28
  83.4 0.6 fusion.5
  84.0 1.2 %fusion.9 = bf16[2,256,192]{1,2,0:T(8,128)(2,1)S(1)} fusion(f32[2,256,1024]{2,1,0:T(8,128)S(1)} %get-tuple-element.8, bf16[2,1024,384]{2,1,0:T(8,128)(2,1)S(1)} %copy-done.6, f32[2,256]{1,0:T(2,128)S(1)} %broadcast_maximum_fusion, pred[2,1024]{1,0:T(4,128)(4,1)S(1)} %bitcast.42, f32[2,256]{1,0:T(2,128)S(1)} %fusion.5), kind=kOutput, calls=%fused_computation.18 | convolution fusion | flops 204144640 | bytes 3350528 | tf_op jit(solution)/shard_map/srk,skd->srd/dot_general | solution.py:36
  85.2 0.1 copy.25
  85.3 0.3 reshape.42
  85.6 0.6 multiply_reduce_fusion
  86.2 0.2 multiply_convert_fusion
  86.4 3.4 %fusion.31 = bf16[64,1536]{1,0:T(8,128)(2,1)S(1)} fusion(bf16[1536,1536]{1,0:T(8,128)(2,1)} %param.17, bf16[2,64,1536]{2,1,0:T(8,128)(2,1)S(1)} %multiply_convert_fusion, f32[1536]{0:T(1024)S(1)} %copy-done.1), kind=kOutput, calls=%fused_computation.42 | convolution fusion | flops 302776320 | bytes 5120000 | tf_op jit(solution)/shard_map/dot_general | solution.py:100
  89.8 4.7 %add_multiply_fusion = f32[64,1536]{1,0:T(8,128)} fusion(bf16[1536,1536]{1,0:T(8,128)(2,1)} %gather_fusion, bf16[64,1536]{1,0:T(8,128)(2,1)S(1)} %fusion.31, bf16[2,64,1536]{2,1,0:T(8,128)(2,1)S(1)} %multiply_convert_fusion, f32[1536]{0:T(1024)S(1)} %gather_fusion.1), kind=kOutput, calls=%fused_computation.48 | convolution fusion | flops 303169536 | bytes 5513216 | tf_op jit(solution)/shard_map/dot_general | solution.py:103
  (31 shorter events, 0.1 us)
Async XLA Ops:
  6.5 79.1 %copy-start = (bf16[768,1536]{1,0:T(8,128)(2,1)S(1)}, bf16[768,1536]{1,0:T(8,128)(2,1)}, u32[]{:S(2)}) copy-start(bf16[768,1536]{1,0:T(8,128)(2,1)} %param.15) | copy-start | bytes 7077892
  6.5 5.7 %copy-start.2 = (bf16[2,64,1536]{2,1,0:T(8,128)(2,1)S(1)}, bf16[2,64,1536]{2,1,0:T(8,128)(2,1)}, u32[]{:S(2)}) copy-start(bf16[2,64,1536]{2,1,0:T(8,128)(2,1)} %param.10) | copy-start | bytes 1179652
  6.5 10.2 %copy-start.7 = (s32[2,64]{1,0:T(2,128)S(1)}, s32[2,64]{1,0:T(2,128)}, u32[]{:S(2)}) copy-start(s32[2,64]{1,0:T(2,128)} %param.11) | copy-start | bytes 1540
  6.5 30.9 %copy-start.4 = (s32[1536]{0:T(1024)S(1)}, s32[1536]{0:T(1024)}, u32[]{:S(2)}) copy-start(s32[1536]{0:T(1024)} %param.19) | copy-start | bytes 18436
  6.5 74.8 %all-gather.3.cloned.1.call-start = ((), (), s32[]{:S(2)}) async-start(), calls=%async_computation | async-start | bytes 1671168 | tf_op jit(solution)/shard_map/all_gather | solution.py:86
  9.8 45.9 %copy-start.3 = (bf16[2,64,1536]{2,1,0:T(8,128)(2,1)}, bf16[2,64,1536]{2,1,0:T(8,128)(2,1)S(1)}, u32[]{:S(2)}) copy-start(bf16[2,64,1536]{2,1,0:T(8,128)(2,1)S(1)} %fusion.27) | copy-start | bytes 1179652
  12.3 1.6 %collective-permute-start = (bf16[64,1536]{1,0:T(8,128)(2,1)S(1)}, bf16[64,1536]{1,0:T(8,128)(2,1)S(1)}, u32[]{:S(2)}, u32[]{:S(2)}) collective-permute-start(bf16[64,1536]{1,0:T(8,128)(2,1)S(1)} %get-tuple-element.6), channel_id=1, source_target_pairs={{0,1},{1,0},{2,3},{3,2},{4,5},{5,4},{6,7},{7,6},{8,9},{9,8},{10,11... | collective-permute-start | bytes 589832 | tf_op jit(solution)/shard_map/ppermute | solution.py:11
  13.9 23.5 %collective-permute-start.1 = (bf16[64,1536]{1,0:T(8,128)(2,1)S(1)}, bf16[64,1536]{1,0:T(8,128)(2,1)S(1)}, u32[]{:S(2)}, u32[]{:S(2)}) collective-permute-start(bf16[64,1536]{1,0:T(8,128)(2,1)S(1)} %collective-permute-done), channel_id=1, source_target_pairs={{0,2},{1,3},{2,0},{3,1},{4,6},{5,7},{6,4},{7,5},{8,10},{9,11},{10,... | collective-permute-start | bytes 589832 | tf_op jit(solution)/shard_map/ppermute | solution.py:11
  37.4 11.5 %collective-permute-start.2 = (bf16[64,1536]{1,0:T(8,128)(2,1)S(1)}, bf16[64,1536]{1,0:T(8,128)(2,1)}, u32[]{:S(2)}, u32[]{:S(2)}) collective-permute-start(bf16[64,1536]{1,0:T(8,128)(2,1)S(1)} %collective-permute-done.1), channel_id=1, source_target_pairs={{0,4},{1,5},{2,6},{3,7},{4,0},{5,1},{6,2},{7,3},{8,12},{9,13},{10,... | collective-permute-start | bytes 589832 | tf_op jit(solution)/shard_map/ppermute | solution.py:11
  48.9 28.7 %collective-permute-start.3 = (bf16[64,1536]{1,0:T(8,128)(2,1)}, bf16[64,1536]{1,0:T(8,128)(2,1)S(1)}, u32[]{:S(2)}, u32[]{:S(2)}) collective-permute-start(bf16[64,1536]{1,0:T(8,128)(2,1)} %collective-permute-done.2), channel_id=1, source_target_pairs={{0,8},{1,9},{2,10},{3,11},{4,12},{5,13},{6,14},{7,15},{8,0},{9,1},... | collective-permute-start | bytes 589832 | tf_op jit(solution)/shard_map/ppermute | solution.py:11
  48.9 6.8 %copy-start.5 = (bf16[1536]{0:T(1024)(128)(2,1)S(1)}, bf16[1536]{0:T(1024)(128)(2,1)}, u32[]{:S(2)}) copy-start(bf16[1536]{0:T(1024)(128)(2,1)} %param.16) | copy-start | bytes 9220
  55.8 13.4 %copy-start.1 = (f32[1536]{0:T(1024)S(1)}, f32[1536]{0:T(1024)}, u32[]{:S(2)}) copy-start(f32[1536]{0:T(1024)} %param.18) | copy-start | bytes 18436
  69.2 9.0 %slice-start = ((bf16[2,64,1536]{2,1,0:T(8,128)(2,1)}), bf16[1,64,1536]{2,1,0:T(8,128)(2,1)S(1)}, s32[]{:S(2)}) async-start(bf16[2,64,1536]{2,1,0:T(8,128)(2,1)} %copy-done.3), calls=%async_computation.1 | async-start | bytes 393216 | tf_op jit(solution)/shard_map/slice | solution.py:71
  81.3 2.7 %copy-start.6 = (bf16[2,1024,384]{2,1,0:T(8,128)(2,1)S(1)}, bf16[2,1024,384]{2,1,0:T(8,128)(2,1)}, u32[]{:S(2)}) copy-start(bf16[2,1024,384]{2,1,0:T(8,128)(2,1)} %all-gather.3.cloned.1.call-done) | copy-start | bytes 4718596
Sparse Core Ops, SparseCore 0:
  12.3 45.7 all-gather.2
where the time goes:
time: 102 us; the launch traced here: 101 us
  local copies, waits for them, and re-layouts  30.3 us (30%)
  blocking collectives  20.7 us (20%)
  matrix products  16.5 us (16%)
  between operations  13.6 us (13%)
  waiting for transfers between devices  12.6 us (12%)
  other arithmetic  4.27 us (4%)
  starting transfers between devices  3.44 us (3%)
    all_gather x1, blocking collectives, per_device(): lax.all_gather(usable_flag, 'tok', axis=1, tiled=True)  20.7 us
    gather x1, local copies, waits for them, and re-layouts, per_device(): head_weight[:, track_perm]  13.4 us
    ppermute x4, waiting for transfers between devices, swapped(): return lax.ppermute(value, axis, pairs)  12.5 us
    gather x1, local copies, waits for them, and re-layouts, per_device(): head_bias[track_perm]  8.38 us
    unnamed x17, local copies, waits for them, and re-layouts  6.77 us
    dot_general x1, matrix products, per_device(): jnp.dot(normed_out[1], head_weight[:, track_perm], preferred_element_type...  4.69 us
    dot_general x1, matrix products, per_device(): jnp.dot(normed_out[0], head_weight, preferred_element_type=jnp.float32)  3.42 us
    ppermute x4, starting transfers between devices, swapped(): return lax.ppermute(value, axis, pairs)  3.41 us
  transfers between devices with their start and end apart: 5, of which 2 were waited for; matrix products, arithmetic and copies ran while one was open for 32% of the time, Pallas kernels for 0%

commit v1 on v0

--- a/solution.py
+++ b/solution.py
@@ -3,6 +3,18 @@
 import jax.numpy as jnp
 from jax import lax
 from jax.sharding import PartitionSpec as P
+
+
+def ring_gather(value, axis, dim):
+    ways, here, step = (lax.axis_size(axis), lax.axis_index(axis), value.shape[dim])
+    dims = [n * ways if d == dim else n for d, n in enumerate(value.shape)]
+    full = lax.dynamic_update_slice_in_dim(
+        jnp.zeros(dims, value.dtype), value, here * step, axis=dim
+    )
+    for far in range(1, ways):
+        value = lax.ppermute(value, axis, [(d, (d + 1) % ways) for d in range(ways)])
+        full = lax.dynamic_update_slice_in_dim(full, value, (here - far) % ways * step, axis=dim)
+    return full
 
 
 def swapped(value, axis, distance):
@@ -84,7 +96,7 @@
         start_state,
         queries,
         lax.all_gather(key_value, "tok", axis=1, tiled=True),
-        lax.all_gather(usable_flag, "tok", axis=1, tiled=True),
+        ring_gather(usable_flag, "tok", 1),
     )
     maxima, totals, accumulated = softmax_state
     attended = (

time: 102 us -> 154 us (1.51)
  waiting for transfers between devices: 12.6 us -> 80.4 us
  blocking collectives: 20.7 us -> 0 us
  local copies, waits for them, and re-layouts: 30.3 us -> 33.2 us
  starting transfers between devices: 3.44 us -> 5.25 us
    ppermute x0 -> x15, waiting for transfers between devices: none -> 67.1 us  [ring_gather(): lax.ppermute(value, axis, [(d, (d + 1) % ways) for d in range(ways)])]
    all_gather x1 -> x0, blocking collectives: 20.7 us -> none  [per_device(): lax.all_gather(usable_flag, 'tok', axis=1, tiled=True)]
    dynamic_update_slice x0 -> x16, local copies, waits for them, and re-layouts: none -> 2.98 us  [the longest x15 2.82 us: ring_gather(): lax.dynamic_update_slice_in_dim(full, value, (here - far) % ways * step,...]
    ppermute x4, starting transfers between devices: 3.41 us -> 5.04 us  [swapped(): return lax.ppermute(value, axis, pairs)]
  transfers between devices with their start and end apart: 5 -> 20, of which waited for: 2 -> 15; matrix products, arithmetic and copies ran while one was open for 32% -> 23% of each run, Pallas kernels for 0% -> 0%
where the time goes in v1:
time: 154 us
  waiting for transfers between devices  80.4 us (52%)
  local copies, waits for them, and re-layouts  33.2 us (22%)
  matrix products  16.5 us (11%)
  between operations  13.7 us (9%)
  starting transfers between devices  5.25 us (3%)
  other arithmetic  4.95 us (3%)
    ppermute x15, waiting for transfers between devices, ring_gather(): lax.ppermute(value, axis, [(d, (d + 1) % ways) for d in range(ways)])  67.1 us
    gather x1, local copies, waits for them, and re-layouts, per_device(): head_weight[:, track_perm]  13.3 us
    ppermute x4, waiting for transfers between devices, swapped(): return lax.ppermute(value, axis, pairs)  13.3 us
    gather x1, local copies, waits for them, and re-layouts, per_device(): head_bias[track_perm]  8.38 us
    unnamed x17, local copies, waits for them, and re-layouts  6.77 us
    ppermute x4, starting transfers between devices, swapped(): return lax.ppermute(value, axis, pairs)  5.04 us
    dot_general x1, matrix products, per_device(): jnp.dot(normed_out[1], head_weight[:, track_perm], preferred_element_type...  4.69 us
    dot_general x1, matrix products, per_device(): jnp.dot(normed_out[0], head_weight, preferred_element_type=jnp.float32)  3.42 us
  transfers between devices with their start and end apart: 20, of which 15 were waited for; matrix products, arithmetic and copies ran while one was open for 23% of the time, Pallas kernels for 0%

profile of v1, /device:TPU:0, one launch (start us, length us, event | category | flops | bytes accessed | tf_op | source)
XLA Modules:
  0.0 153.9 jit_solution(3906463291871808619)
XLA Ops:
  6.6 0.8 convert_element_type.55
  7.4 1.2 fusion.25
  8.6 1.2 fusion.27
  9.8 2.4 %fusion.13 = bf16[2,64,384]{2,1,0:T(8,128)(2,1)} fusion(bf16[2,64,1536]{2,1,0:T(8,128)(2,1)S(1)} %fusion.27, bf16[1536,384]{1,0:T(8,128)(2,1)} %param.14), kind=kOutput, calls=%fused_computation.20 | convolution fusion | flops 151044096 | bytes 1671168 | tf_op jit(solution)/shard_map/std,de->ste/dot_general | solution.py:75
  12.9 1.0 collective-permute-done
  13.9 2.8 %collective-permute-start.1 = (bf16[64,1536]{1,0:T(8,128)(2,1)S(1)}, bf16[64,1536]{1,0:T(8,128)(2,1)S(1)}, u32[]{:S(2)}, u32[]{:S(2)}) collective-permute-start(bf16[64,1536]{1,0:T(8,128)(2,1)S(1)} %collective-permute-done), channel_id=1, source_target_pairs={{0,2},{1,3},{2,0},{3,1},{4,6},{5,7},{6,4},{7,5},{8,10},{9,11},{10,... | collective-permute-start | bytes 589832 | tf_op jit(solution)/shard_map/ppermute | solution.py:23
  16.7 5.6 %collective-permute-done.1 = bf16[64,1536]{1,0:T(8,128)(2,1)S(1)} collective-permute-done((bf16[64,1536]{1,0:T(8,128)(2,1)S(1)}, bf16[64,1536]{1,0:T(8,128)(2,1)S(1)}, u32[]{:S(2)}, u32[]{:S(2)}) %collective-permute-start.1) | collective-permute-done | bytes 196640 | tf_op jit(solution)/shard_map/ppermute | solution.py:23
  22.3 1.6 %collective-permute-start.2 = (bf16[64,1536]{1,0:T(8,128)(2,1)S(1)}, bf16[64,1536]{1,0:T(8,128)(2,1)}, u32[]{:S(2)}, u32[]{:S(2)}) collective-permute-start(bf16[64,1536]{1,0:T(8,128)(2,1)S(1)} %collective-permute-done.1), channel_id=1, source_target_pairs={{0,4},{1,5},{2,6},{3,7},{4,0},{5,1},{6,2},{7,3},{8,12},{9,13},{10,... | collective-permute-start | bytes 589832 | tf_op jit(solution)/shard_map/ppermute | solution.py:23
  23.9 0.7 fusion.47
  24.6 7.4 %collective-permute-done.5 = bf16[2,64]{1,0:T(2,128)(2,1)S(1)} collective-permute-done((bf16[2,64]{1,0:T(2,128)(2,1)S(1)}, bf16[2,64]{1,0:T(2,128)(2,1)S(1)}, u32[]{:S(2)}, u32[]{:S(2)}) %collective-permute-start.5) | collective-permute-done | bytes 288 | tf_op jit(solution)/shard_map/ppermute | solution.py:15
  32.0 5.7 %collective-permute-done.6 = bf16[2,64]{1,0:T(2,128)(2,1)S(1)} collective-permute-done((bf16[2,64]{1,0:T(2,128)(2,1)S(1)}, bf16[2,64]{1,0:T(2,128)(2,1)S(1)}, u32[]{:S(2)}, u32[]{:S(2)}) %collective-permute-start.6) | collective-permute-done | bytes 288 | tf_op jit(solution)/shard_map/ppermute | solution.py:15
  37.7 5.7 %collective-permute-done.7 = bf16[2,64]{1,0:T(2,128)(2,1)S(1)} collective-permute-done((bf16[2,64]{1,0:T(2,128)(2,1)S(1)}, bf16[2,64]{1,0:T(2,128)(2,1)S(1)}, u32[]{:S(2)}, u32[]{:S(2)}) %collective-permute-start.7) | collective-permute-done | bytes 288 | tf_op jit(solution)/shard_map/ppermute | solution.py:15
  43.4 5.7 %collective-permute-done.8 = bf16[2,64]{1,0:T(2,128)(2,1)S(1)} collective-permute-done((bf16[2,64]{1,0:T(2,128)(2,1)S(1)}, bf16[2,64]{1,0:T(2,128)(2,1)S(1)}, u32[]{:S(2)}, u32[]{:S(2)}) %collective-permute-start.8) | collective-permute-done | bytes 288 | tf_op jit(solution)/shard_map/ppermute | solution.py:15
  49.1 6.7 %copy.19 = bf16[1536,1536]{0,1:T(8,128)(2,1)} copy(bf16[1536,1536]{1,0:T(8,128)(2,1)} %param.17) | data formatting | bytes 9437184 | tf_op args[7]
  55.8 13.3 %gather_fusion = bf16[1536,1536]{1,0:T(8,128)(2,1)} fusion(bf16[1536,1536]{0,1:T(8,128)(2,1)} %copy.19, s32[2048]{0:T(1024)S(1)} %pad_clamp_fusion), kind=kCustom, calls=%fused_computation | custom fusion | bytes 9443328 | tf_op jit(solution)/shard_map/gather | solution.py:115
  69.2 8.4 %gather_fusion.1 = f32[1536]{0:T(1024)S(1)} fusion(f32[1536]{0:T(1024)S(1)} %copy-done.1, s32[2048]{0:T(1024)S(1)} %pad_clamp_fusion), kind=kCustom, calls=%fused_computation.1 | custom fusion | bytes 18432 | tf_op jit(solution)/shard_map/gather | solution.py:116
  77.7 5.6 %collective-permute-done.11 = bf16[2,64]{1,0:T(2,128)(2,1)S(1)} collective-permute-done((bf16[2,64]{1,0:T(2,128)(2,1)S(1)}, bf16[2,64]{1,0:T(2,128)(2,1)S(1)}, u32[]{:S(2)}, u32[]{:S(2)}) %collective-permute-start.11) | collective-permute-done | bytes 288 | tf_op jit(solution)/shard_map/ppermute | solution.py:15
  83.3 5.7 %collective-permute-done.12 = bf16[2,64]{1,0:T(2,128)(2,1)S(1)} collective-permute-done((bf16[2,64]{1,0:T(2,128)(2,1)S(1)}, bf16[2,64]{1,0:T(2,128)(2,1)S(1)}, u32[]{:S(2)}, u32[]{:S(2)}) %collective-permute-start.12) | collective-permute-done | bytes 288 | tf_op jit(solution)/shard_map/ppermute | solution.py:15
  89.0 5.7 %collective-permute-done.13 = bf16[2,64]{1,0:T(2,128)(2,1)S(1)} collective-permute-done((bf16[2,64]{1,0:T(2,128)(2,1)S(1)}, bf16[2,64]{1,0:T(2,128)(2,1)S(1)}, u32[]{:S(2)}, u32[]{:S(2)}) %collective-permute-start.13) | collective-permute-done | bytes 288 | tf_op jit(solution)/shard_map/ppermute | solution.py:15
  95.3 5.1 %collective-permute-done.14 = bf16[2,64]{1,0:T(2,128)(2,1)S(1)} collective-permute-done((bf16[2,64]{1,0:T(2,128)(2,1)S(1)}, bf16[2,64]{1,0:T(2,128)(2,1)S(1)}, u32[]{:S(2)}, u32[]{:S(2)}) %collective-permute-start.14) | collective-permute-done | bytes 288 | tf_op jit(solution)/shard_map/ppermute | solution.py:15
  101.0 5.1 %collective-permute-done.15 = bf16[2,64]{1,0:T(2,128)(2,1)S(1)} collective-permute-done((bf16[2,64]{1,0:T(2,128)(2,1)S(1)}, bf16[2,64]{1,0:T(2,128)(2,1)S(1)}, u32[]{:S(2)}, u32[]{:S(2)}) %collective-permute-start.15) | collective-permute-done | bytes 288 | tf_op jit(solution)/shard_map/ppermute | solution.py:15
  106.6 5.2 %collective-permute-done.16 = bf16[2,64]{1,0:T(2,128)(2,1)S(1)} collective-permute-done((bf16[2,64]{1,0:T(2,128)(2,1)S(1)}, bf16[2,64]{1,0:T(2,128)(2,1)S(1)}, u32[]{:S(2)}, u32[]{:S(2)}) %collective-permute-start.16) | collective-permute-done | bytes 288 | tf_op jit(solution)/shard_map/ppermute | solution.py:15
  112.4 5.1 %collective-permute-done.17 = bf16[2,64]{1,0:T(2,128)(2,1)S(1)} collective-permute-done((bf16[2,64]{1,0:T(2,128)(2,1)S(1)}, bf16[2,64]{1,0:T(2,128)(2,1)S(1)}, u32[]{:S(2)}, u32[]{:S(2)}) %collective-permute-start.17) | collective-permute-done | bytes 288 | tf_op jit(solution)/shard_map/ppermute | solution.py:15
  118.0 5.2 %collective-permute-done.18 = bf16[2,64]{1,0:T(2,128)(2,1)S(1)} collective-permute-done((bf16[2,64]{1,0:T(2,128)(2,1)S(1)}, bf16[2,64]{1,0:T(2,128)(2,1)S(1)}, u32[]{:S(2)}, u32[]{:S(2)}) %collective-permute-start.18) | collective-permute-done | bytes 288 | tf_op jit(solution)/shard_map/ppermute | solution.py:15
  123.5 6.7 %collective-permute-done.3 = bf16[64,1536]{1,0:T(8,128)(2,1)S(1)} collective-permute-done((bf16[64,1536]{1,0:T(8,128)(2,1)}, bf16[64,1536]{1,0:T(8,128)(2,1)S(1)}, u32[]{:S(2)}, u32[]{:S(2)}) %collective-permute-start.3) | collective-permute-done | bytes 196640 | tf_op jit(solution)/shard_map/ppermute | solution.py:23
  130.8 2.2 %fusion.10 = bf16[2,64,768]{2,1,0:T(8,128)(2,1)S(1)} fusion(bf16[1536,768]{1,0:T(8,128)(2,1)} %param.13, bf16[1,64,1536]{2,1,0:T(8,128)(2,1)S(1)} %fusion.36, bf16[1,64,1536]{2,1,0:T(8,128)(2,1)S(1)} %slice-done), kind=kOutput, calls=%fused_computation.19 | convolution fusion | flops 302284800 | bytes 2949120 | tf_op jit(solution)/shard_map/std,de->ste/dot_general | solution.py:85
  133.0 1.0 reshape.71
  134.0 2.0 %fusion.4 = (f32[2,256]{1,0:T(2,128)S(1)}, f32[2,256,1024]{2,1,0:T(8,128)S(1)}) fusion(pred[2,1024]{1,0:T(4,128)(4,1)S(1)} %compare_bitcast_fusion, bf16[2,256,192]{2,1,0:T(8,128)(2,1)} %reshape.71, bf16[2,1024,384]{2,1,0:T(8,128)(2,1)} %all-gather.2.cloned.1.call-done), kind=kOutput, calls=%fused_computation.10 | convolution fusion | flops 202898944 | bytes 3411968 | tf_op jit(solution)/shard_map/srd,skd->srk/dot_general | solution.py:40
  136.0 0.6 fusion.5
  136.6 1.2 fusion.9
  139.0 3.4 %fusion.31 = bf16[64,1536]{1,0:T(8,128)(2,1)S(1)} fusion(bf16[1536,1536]{1,0:T(8,128)(2,1)} %param.17, bf16[2,64,1536]{2,1,0:T(8,128)(2,1)S(1)} %multiply_convert_fusion, f32[1536]{0:T(1024)S(1)} %copy-done.1), kind=kOutput, calls=%fused_computation.42 | convolution fusion | flops 302776320 | bytes 5120000 | tf_op jit(solution)/shard_map/dot_general | solution.py:112
  142.4 4.7 %add_multiply_fusion = f32[64,1536]{1,0:T(8,128)} fusion(bf16[1536,1536]{1,0:T(8,128)(2,1)} %gather_fusion, bf16[64,1536]{1,0:T(8,128)(2,1)S(1)} %fusion.31, bf16[2,64,1536]{2,1,0:T(8,128)(2,1)S(1)} %multiply_convert_fusion, f32[1536]{0:T(1024)S(1)} %gather_fusion.1), kind=kOutput, calls=%fused_computation.48 | convolution fusion | flops 303169536 | bytes 5513216 | tf_op jit(solution)/shard_map/dot_general | solution.py:115
  (76 shorter events, 5.7 us)
Async XLA Ops:
  6.5 131.7 %copy-start = (bf16[768,1536]{1,0:T(8,128)(2,1)S(1)}, bf16[768,1536]{1,0:T(8,128)(2,1)}, u32[]{:S(2)}) copy-start(bf16[768,1536]{1,0:T(8,128)(2,1)} %param.15) | copy-start | bytes 7077892
  6.5 5.7 %copy-start.2 = (bf16[2,64,1536]{2,1,0:T(8,128)(2,1)S(1)}, bf16[2,64,1536]{2,1,0:T(8,128)(2,1)}, u32[]{:S(2)}) copy-start(bf16[2,64,1536]{2,1,0:T(8,128)(2,1)} %param.10) | copy-start | bytes 1179652
  6.5 6.3 %copy-start.7 = (s32[2,64]{1,0:T(2,128)S(1)}, s32[2,64]{1,0:T(2,128)}, u32[]{:S(2)}) copy-start(s32[2,64]{1,0:T(2,128)} %param.11) | copy-start | bytes 1540
  6.5 10.2 %copy-start.4 = (s32[1536]{0:T(1024)S(1)}, s32[1536]{0:T(1024)}, u32[]{:S(2)}) copy-start(s32[1536]{0:T(1024)} %param.19) | copy-start | bytes 18436
  6.5 127.4 %all-gather.2.cloned.1.call-start = ((), (), s32[]{:S(2)}) async-start(), calls=%async_computation | async-start | bytes 1671168 | tf_op jit(solution)/shard_map/all_gather | solution.py:98
  9.8 46.0 %copy-start.3 = (bf16[2,64,1536]{2,1,0:T(8,128)(2,1)}, bf16[2,64,1536]{2,1,0:T(8,128)(2,1)S(1)}, u32[]{:S(2)}) copy-start(bf16[2,64,1536]{2,1,0:T(8,128)(2,1)S(1)} %fusion.27) | copy-start | bytes 1179652
  12.3 1.6 %collective-permute-start = (bf16[64,1536]{1,0:T(8,128)(2,1)S(1)}, bf16[64,1536]{1,0:T(8,128)(2,1)S(1)}, u32[]{:S(2)}, u32[]{:S(2)}) collective-permute-start(bf16[64,1536]{1,0:T(8,128)(2,1)S(1)} %get-tuple-element.6), channel_id=1, source_target_pairs={{0,1},{1,0},{2,3},{3,2},{4,5},{5,4},{6,7},{7,6},{8,9},{9,8},{10,11... | collective-permute-start | bytes 589832 | tf_op jit(solution)/shard_map/ppermute | solution.py:23
  12.8 11.7 %collective-permute-start.4 = (bf16[2,64]{1,0:T(2,128)(2,1)S(1)}, bf16[2,64]{1,0:T(2,128)(2,1)S(1)}, u32[]{:S(2)}, u32[]{:S(2)}) collective-permute-start(bf16[2,64]{1,0:T(2,128)(2,1)S(1)} %compare_convert_fusion), channel_id=1, source_target_pairs={{0,1},{1,2},{2,3},{3,4},{4,5},{5,6},{6,7},{7,8},{8,9},{9,10},{10,1... | collective-permute-start | bytes 776 | tf_op jit(solution)/shard_map/ppermute | solution.py:15
  13.9 8.4 %collective-permute-start.1 = (bf16[64,1536]{1,0:T(8,128)(2,1)S(1)}, bf16[64,1536]{1,0:T(8,128)(2,1)S(1)}, u32[]{:S(2)}, u32[]{:S(2)}) collective-permute-start(bf16[64,1536]{1,0:T(8,128)(2,1)S(1)} %collective-permute-done), channel_id=1, source_target_pairs={{0,2},{1,3},{2,0},{3,1},{4,6},{5,7},{6,4},{7,5},{8,10},{9,11},{10,... | collective-permute-start | bytes 589832 | tf_op jit(solution)/shard_map/ppermute | solution.py:23
  22.3 101.1 %collective-permute-start.2 = (bf16[64,1536]{1,0:T(8,128)(2,1)S(1)}, bf16[64,1536]{1,0:T(8,128)(2,1)}, u32[]{:S(2)}, u32[]{:S(2)}) collective-permute-start(bf16[64,1536]{1,0:T(8,128)(2,1)S(1)} %collective-permute-done.1), channel_id=1, source_target_pairs={{0,4},{1,5},{2,6},{3,7},{4,0},{5,1},{6,2},{7,3},{8,12},{9,13},{10,... | collective-permute-start | bytes 589832 | tf_op jit(solution)/shard_map/ppermute | solution.py:23
  24.6 7.4 %collective-permute-start.5 = (bf16[2,64]{1,0:T(2,128)(2,1)S(1)}, bf16[2,64]{1,0:T(2,128)(2,1)S(1)}, u32[]{:S(2)}, u32[]{:S(2)}) collective-permute-start(bf16[2,64]{1,0:T(2,128)(2,1)S(1)} %collective-permute-done.4), channel_id=1, source_target_pairs={{0,1},{1,2},{2,3},{3,4},{4,5},{5,6},{6,7},{7,8},{8,9},{9,10},{10,1... | collective-permute-start | bytes 776 | tf_op jit(solution)/shard_map/ppermute | solution.py:15
  32.0 5.7 %collective-permute-start.6 = (bf16[2,64]{1,0:T(2,128)(2,1)S(1)}, bf16[2,64]{1,0:T(2,128)(2,1)S(1)}, u32[]{:S(2)}, u32[]{:S(2)}) collective-permute-start(bf16[2,64]{1,0:T(2,128)(2,1)S(1)} %collective-permute-done.5), channel_id=1, source_target_pairs={{0,1},{1,2},{2,3},{3,4},{4,5},{5,6},{6,7},{7,8},{8,9},{9,10},{10,1... | collective-permute-start | bytes 776 | tf_op jit(solution)/shard_map/ppermute | solution.py:15
  37.6 5.7 %collective-permute-start.7 = (bf16[2,64]{1,0:T(2,128)(2,1)S(1)}, bf16[2,64]{1,0:T(2,128)(2,1)S(1)}, u32[]{:S(2)}, u32[]{:S(2)}) collective-permute-start(bf16[2,64]{1,0:T(2,128)(2,1)S(1)} %collective-permute-done.6), channel_id=1, source_target_pairs={{0,1},{1,2},{2,3},{3,4},{4,5},{5,6},{6,7},{7,8},{8,9},{9,10},{10,1... | collective-permute-start | bytes 776 | tf_op jit(solution)/shard_map/ppermute | solution.py:15
  43.3 5.7 %collective-permute-start.8 = (bf16[2,64]{1,0:T(2,128)(2,1)S(1)}, bf16[2,64]{1,0:T(2,128)(2,1)S(1)}, u32[]{:S(2)}, u32[]{:S(2)}) collective-permute-start(bf16[2,64]{1,0:T(2,128)(2,1)S(1)} %collective-permute-done.7), channel_id=1, source_target_pairs={{0,1},{1,2},{2,3},{3,4},{4,5},{5,6},{6,7},{7,8},{8,9},{9,10},{10,1... | collective-permute-start | bytes 776 | tf_op jit(solution)/shard_map/ppermute | solution.py:15
  49.0 6.8 %collective-permute-start.9 = (bf16[2,64]{1,0:T(2,128)(2,1)S(1)}, bf16[2,64]{1,0:T(2,128)(2,1)S(1)}, u32[]{:S(2)}, u32[]{:S(2)}) collective-permute-start(bf16[2,64]{1,0:T(2,128)(2,1)S(1)} %collective-permute-done.8), channel_id=1, source_target_pairs={{0,1},{1,2},{2,3},{3,4},{4,5},{5,6},{6,7},{7,8},{8,9},{9,10},{10,1... | collective-permute-start | bytes 776 | tf_op jit(solution)/shard_map/ppermute | solution.py:15
  49.1 6.8 %copy-start.5 = (bf16[1536]{0:T(1024)(128)(2,1)S(1)}, bf16[1536]{0:T(1024)(128)(2,1)}, u32[]{:S(2)}) copy-start(bf16[1536]{0:T(1024)(128)(2,1)} %param.16) | copy-start | bytes 9220
  55.8 21.8 %collective-permute-start.10 = (bf16[2,64]{1,0:T(2,128)(2,1)S(1)}, bf16[2,64]{1,0:T(2,128)(2,1)S(1)}, u32[]{:S(2)}, u32[]{:S(2)}) collective-permute-start(bf16[2,64]{1,0:T(2,128)(2,1)S(1)} %collective-permute-done.9), channel_id=1, source_target_pairs={{0,1},{1,2},{2,3},{3,4},{4,5},{5,6},{6,7},{7,8},{8,9},{9,10},{10,1... | collective-permute-start | bytes 776 | tf_op jit(solution)/shard_map/ppermute | solution.py:15
  55.8 13.4 %copy-start.1 = (f32[1536]{0:T(1024)S(1)}, f32[1536]{0:T(1024)}, u32[]{:S(2)}) copy-start(f32[1536]{0:T(1024)} %param.18) | copy-start | bytes 18436
  69.2 61.6 %slice-start = ((bf16[2,64,1536]{2,1,0:T(8,128)(2,1)}), bf16[1,64,1536]{2,1,0:T(8,128)(2,1)S(1)}, s32[]{:S(2)}) async-start(bf16[2,64,1536]{2,1,0:T(8,128)(2,1)} %copy-done.3), calls=%async_computation.1 | async-start | bytes 393216 | tf_op jit(solution)/shard_map/slice | solution.py:83
  77.6 5.7 %collective-permute-start.11 = (bf16[2,64]{1,0:T(2,128)(2,1)S(1)}, bf16[2,64]{1,0:T(2,128)(2,1)S(1)}, u32[]{:S(2)}, u32[]{:S(2)}) collective-permute-start(bf16[2,64]{1,0:T(2,128)(2,1)S(1)} %collective-permute-done.10), channel_id=1, source_target_pairs={{0,1},{1,2},{2,3},{3,4},{4,5},{5,6},{6,7},{7,8},{8,9},{9,10},{10,1... | collective-permute-start | bytes 776 | tf_op jit(solution)/shard_map/ppermute | solution.py:15
  83.3 5.7 %collective-permute-start.12 = (bf16[2,64]{1,0:T(2,128)(2,1)S(1)}, bf16[2,64]{1,0:T(2,128)(2,1)S(1)}, u32[]{:S(2)}, u32[]{:S(2)}) collective-permute-start(bf16[2,64]{1,0:T(2,128)(2,1)S(1)} %collective-permute-done.11), channel_id=1, source_target_pairs={{0,1},{1,2},{2,3},{3,4},{4,5},{5,6},{6,7},{7,8},{8,9},{9,10},{10,1... | collective-permute-start | bytes 776 | tf_op jit(solution)/shard_map/ppermute | solution.py:15
  89.0 5.7 %collective-permute-start.13 = (bf16[2,64]{1,0:T(2,128)(2,1)S(1)}, bf16[2,64]{1,0:T(2,128)(2,1)S(1)}, u32[]{:S(2)}, u32[]{:S(2)}) collective-permute-start(bf16[2,64]{1,0:T(2,128)(2,1)S(1)} %collective-permute-done.12), channel_id=1, source_target_pairs={{0,1},{1,2},{2,3},{3,4},{4,5},{5,6},{6,7},{7,8},{8,9},{9,10},{10,1... | collective-permute-start | bytes 776 | tf_op jit(solution)/shard_map/ppermute | solution.py:15
  94.7 5.7 %collective-permute-start.14 = (bf16[2,64]{1,0:T(2,128)(2,1)S(1)}, bf16[2,64]{1,0:T(2,128)(2,1)S(1)}, u32[]{:S(2)}, u32[]{:S(2)}) collective-permute-start(bf16[2,64]{1,0:T(2,128)(2,1)S(1)} %collective-permute-done.13), channel_id=1, source_target_pairs={{0,1},{1,2},{2,3},{3,4},{4,5},{5,6},{6,7},{7,8},{8,9},{9,10},{10,1... | collective-permute-start | bytes 776 | tf_op jit(solution)/shard_map/ppermute | solution.py:15
  100.4 5.7 %collective-permute-start.15 = (bf16[2,64]{1,0:T(2,128)(2,1)S(1)}, bf16[2,64]{1,0:T(2,128)(2,1)S(1)}, u32[]{:S(2)}, u32[]{:S(2)}) collective-permute-start(bf16[2,64]{1,0:T(2,128)(2,1)S(1)} %collective-permute-done.14), channel_id=1, source_target_pairs={{0,1},{1,2},{2,3},{3,4},{4,5},{5,6},{6,7},{7,8},{8,9},{9,10},{10,1... | collective-permute-start | bytes 776 | tf_op jit(solution)/shard_map/ppermute | solution.py:15
  106.1 5.7 %collective-permute-start.16 = (bf16[2,64]{1,0:T(2,128)(2,1)S(1)}, bf16[2,64]{1,0:T(2,128)(2,1)S(1)}, u32[]{:S(2)}, u32[]{:S(2)}) collective-permute-start(bf16[2,64]{1,0:T(2,128)(2,1)S(1)} %collective-permute-done.15), channel_id=1, source_target_pairs={{0,1},{1,2},{2,3},{3,4},{4,5},{5,6},{6,7},{7,8},{8,9},{9,10},{10,1... | collective-permute-start | bytes 776 | tf_op jit(solution)/shard_map/ppermute | solution.py:15
  111.8 5.7 %collective-permute-start.17 = (bf16[2,64]{1,0:T(2,128)(2,1)S(1)}, bf16[2,64]{1,0:T(2,128)(2,1)S(1)}, u32[]{:S(2)}, u32[]{:S(2)}) collective-permute-start(bf16[2,64]{1,0:T(2,128)(2,1)S(1)} %collective-permute-done.16), channel_id=1, source_target_pairs={{0,1},{1,2},{2,3},{3,4},{4,5},{5,6},{6,7},{7,8},{8,9},{9,10},{10,1... | collective-permute-start | bytes 776 | tf_op jit(solution)/shard_map/ppermute | solution.py:15
  117.5 5.7 %collective-permute-start.18 = (bf16[2,64]{1,0:T(2,128)(2,1)S(1)}, bf16[2,64]{1,0:T(2,128)(2,1)S(1)}, u32[]{:S(2)}, u32[]{:S(2)}) collective-permute-start(bf16[2,64]{1,0:T(2,128)(2,1)S(1)} %collective-permute-done.17), channel_id=1, source_target_pairs={{0,1},{1,2},{2,3},{3,4},{4,5},{5,6},{6,7},{7,8},{8,9},{9,10},{10,1... | collective-permute-start | bytes 776 | tf_op jit(solution)/shard_map/ppermute | solution.py:15
  123.4 6.8 %collective-permute-start.3 = (bf16[64,1536]{1,0:T(8,128)(2,1)}, bf16[64,1536]{1,0:T(8,128)(2,1)S(1)}, u32[]{:S(2)}, u32[]{:S(2)}) collective-permute-start(bf16[64,1536]{1,0:T(8,128)(2,1)} %collective-permute-done.2), channel_id=1, source_target_pairs={{0,8},{1,9},{2,10},{3,11},{4,12},{5,13},{6,14},{7,15},{8,0},{9,1},... | collective-permute-start | bytes 589832 | tf_op jit(solution)/shard_map/ppermute | solution.py:23
  134.0 2.7 %copy-start.6 = (bf16[2,1024,384]{2,1,0:T(8,128)(2,1)S(1)}, bf16[2,1024,384]{2,1,0:T(8,128)(2,1)}, u32[]{:S(2)}) copy-start(bf16[2,1024,384]{2,1,0:T(8,128)(2,1)} %all-gather.2.cloned.1.call-done) | copy-start | bytes 4718596
Sparse Core Ops, SparseCore 0:
  12.3 43.2 all-gather.1
